TPU v7x, 32 devices: a whole 2x2x4 slice. The times are simulated.
32 devices in a mesh: gz: 4 (over y, x), phi: 8 (over z, core).
Axes of the slice: x: 2, y: 2, z: 4, core: 2. Of those that a mesh axis runs over, the one named last changes fastest.
Arguments:
- potential_in: float32 [256, 512, 256], P('phi', 'gz'), may hold values from -6 to 6
- charge: float32 [256, 512, 256], P('phi', 'gz'), may hold values from -6 to 6
- cell_kind: int32 [256, 512, 256], P('phi', 'gz'), may hold values from 0 to 2, as said below
Outputs:
- potential: float32 [256, 512, 256], P('phi', 'gz')
- shift_r: float32 [256, 512, 256], P('phi', 'gz')
- shift_rphi: float32 [256, 512, 256], P('phi', 'gz')
Inputs may be any that keep to these rules, and one draw needn't show every extreme that they name: `cell_kind`: 0 marks a free cell, 1 an electrode cell held at zero potential, 2 a boundary cell held at its given potential.
All inputs are finite; a program needn't handle non-finite values.
Results may differ from a plain program's by a relative error of at most 0.000073.
Values sent between devices are 32-bit elements; how exact they have to be, the bound alone decides.
A program may use at most 128 MiB of HBM per device.

v0:
```python
import functools
import math

import jax
import jax.numpy as jnp
import numpy as np
from jax import lax
from jax.experimental import pallas as pl
from jax.experimental.pallas import tpu as pltpu
from jax.sharding import PartitionSpec as P

PASSES = 3
HALVES = 2 * PASSES
RELAX = 1.5
FIXED = 1e30
MESH = pl.DeviceIdType.MESH
PAD = 8
LOAD_PAIRS = 2


def parity_mask(radial):
    row = lax.broadcasted_iota(jnp.int32, (8, radial), 0)
    lane = lax.broadcasted_iota(jnp.int32, (8, radial), 1)
    return (row + lane) % 2 == 0


def relax_kernel(
    slabs, rings, pot, chg, kind, coef, field, carry,
    pot_in, chg_in, kind_in, source, jsend, jrecv, zsend, zrecv, total, total_recv,
    load_sem, jsend_sem, jrecv_sem, zsend_sem, zrecv_sem, tsend_sem, trecv_sem,
):
    pairs = source.shape[1]
    depth = source.shape[2]
    radial = source.shape[3]
    half = depth // 2
    slab = lax.axis_index("gz")
    ring = lax.axis_index("phi")
    right, left = lax.rem(ring + 1, rings), lax.rem(ring + rings - 1, rings)

    chunks = [(0, 1), (pairs - 1, 1)]
    at = 1
    while at < pairs - 1:
        chunks.append((at, min(LOAD_PAIRS, pairs - 1 - at)))
        at += LOAD_PAIRS

    def loads(index):
        first, count = chunks[index]
        part = pl.ds(2 * first, 2 * count)
        return [
            pltpu.make_async_copy(src.at[part], dst.at[part], load_sem.at[index, n])
            for n, (src, dst) in enumerate(((pot, pot_in), (chg, chg_in), (kind, kind_in)))
        ]

    for index in range(len(chunks)):
        for copy in loads(index):
            copy.start()

    barrier = pltpu.get_barrier_semaphore()
    for neighbour in (left, right):
        pl.semaphore_signal(barrier, inc=1, device_id={"phi": neighbour}, device_id_type=MESH)
    for step in range(1, slabs):
        peer = lax.rem(slab + step, slabs)
        pl.semaphore_signal(barrier, inc=1, device_id={"gz": peer}, device_id_type=MESH)

    def prepare(pair):
        mask = parity_mask(radial)
        weight = coef[3]
        for row in range(0, depth, 8):
            rows = pl.ds(row, 8)
            out = pl.ds(row + PAD, 8)
            plane, charges = [], []
            for side in range(2):
                what = kind_in[2 * pair + side, rows, :]
                plane.append(jnp.where(what == 1, 0.0, pot_in[2 * pair + side, rows, :]))
                charges.append(
                    jnp.where(what == 0, weight * chg_in[2 * pair + side, rows, :], FIXED)
                )
            field[0, pair + 1, out, :] = jnp.where(mask, plane[0], plane[1])
            field[1, pair + 1, out, :] = jnp.where(mask, plane[1], plane[0])
            source[0, pair, rows, :] = jnp.where(mask, charges[0], charges[1])
            source[1, pair, rows, :] = jnp.where(mask, charges[1], charges[0])

    def jcopy(turn, side):
        return pltpu.make_async_remote_copy(
            src_ref=jsend.at[turn, side],
            dst_ref=jrecv.at[turn, side],
            send_sem=jsend_sem.at[turn, side],
            recv_sem=jrecv_sem.at[turn, side],
            device_id={"phi": (right, left)[side]},
            device_id_type=MESH,
        )

    def zcopy(turn, side):
        return pltpu.make_async_remote_copy(
            src_ref=zsend.at[turn, side],
            dst_ref=zrecv.at[turn, side],
            send_sem=zsend_sem.at[turn, side],
            recv_sem=zrecv_sem.at[turn, side],
            device_id={"gz": (lax.rem(slab + 1, slabs), lax.rem(slab + slabs - 1, slabs))[side]},
            device_id_type=MESH,
        )

    has_next, has_prev = slab < slabs - 1, slab > 0

    def send_j(turn, color, side):
        pair = (pairs, 1)[side]
        mask = parity_mask(radial)
        first = (color == 1) == (side == 0)
        for row in range(0, half, 8):
            upper = field[color, pair, pl.ds(PAD + row, 8), :]
            lower = pltpu.roll(field[color, pair, pl.ds(PAD + row + half, 8), :], 1, axis=1)
            jsend[turn, side, pl.ds(row, 8), :] = (
                jnp.where(mask, upper, lower) if first else jnp.where(mask, lower, upper)
            )
        jcopy(turn, side).start()

    def take_j(turn, color, side):
        jcopy(turn, side).wait_recv()
        pair = (0, pairs + 1)[side]
        for row in range(0, half, 8):
            face = jrecv[turn, side, pl.ds(row, 8), :]
            field[color, pair, pl.ds(PAD + row, 8), :] = face
            field[color, pair, pl.ds(PAD + row + half, 8), :] = pltpu.roll(face, radial - 1, axis=1)

    def send_z(turn, color):
        for pair in range(pairs):
            zsend[turn, 0, pair] = field[color, pair + 1, pl.ds(PAD + depth - 1, 1), :]
            zsend[turn, 1, pair] = field[color, pair + 1, pl.ds(PAD, 1), :]

        @pl.when(has_next)
        def _():
            zcopy(turn, 0).start()

        @pl.when(has_prev)
        def _():
            zcopy(turn, 1).start()

    def take_z(turn, color):
        @pl.when(has_prev)
        def _():
            zcopy(turn, 0).wait_recv()
            for pair in range(pairs):
                field[color, pair + 1, pl.ds(PAD - 1, 1), :] = zrecv[turn, 0, pair]

        @pl.when(has_next)
        def _():
            zcopy(turn, 1).wait_recv()
            for pair in range(pairs):
                field[color, pair + 1, pl.ds(PAD + depth, 1), :] = zrecv[turn, 1, pair]

    def update(pair, color):
        other = 1 - color
        mask = parity_mask(radial)
        out_c, in_c, around_c, z_c = coef[0], coef[1], coef[2], coef[3]
        before, after = (pair - 1, pair + 1) if color == 0 else (pair + 1, pair - 1)
        for row in range(0, depth, 8):
            rows = pl.ds(row + PAD, 8)
            own = field[color, pair, rows, :]
            near = field[other, pair, rows, :]
            beside = near + jnp.where(mask, field[other, before, rows, :], field[other, after, rows, :])
            along = (
                field[other, pair, pl.ds(row + PAD - 1, 8), :]
                + field[other, pair, pl.ds(row + PAD + 1, 8), :]
            )
            put = source[color, pair - 1, pl.ds(row, 8), :]
            fresh = (
                put
                - (RELAX - 1.0) * own
                + out_c * pltpu.roll(near, radial - 1, axis=1)
                + in_c * pltpu.roll(near, 1, axis=1)
                + around_c * beside
                + z_c * along
            )
            field[color, pair, rows, :] = jnp.where(put < 0.5 * FIXED, fresh, own)

    edge = jnp.zeros((PAD, radial), jnp.float32)
    for color in range(2):
        for pair in range(1, pairs + 1):
            field[color, pair, pl.ds(0, PAD), :] = edge
            field[color, pair, pl.ds(PAD + depth, PAD), :] = edge

    for index in range(2):
        for copy in loads(index):
            copy.wait()
        prepare(chunks[index][0])
    pl.semaphore_wait(barrier, 2 + slabs - 1)
    for side in range(2):
        send_j(0, 1, side)
    for index in range(2, len(chunks)):
        for copy in loads(index):
            copy.wait()
        first, count = chunks[index]
        lax.fori_loop(first, first + count, lambda a, _: (prepare(a), 0)[1], 0)
    send_z(0, 1)

    for turn in range(HALVES):
        color = turn % 2
        take_z(turn, 1 - color)
        for side in range(2):
            take_j(turn, 1 - color, side)
        for side in range(2):
            update((pairs, 1)[side], color)
            send_j(turn + 1, color, side)
        lax.fori_loop(2, pairs, lambda a, _: (update(a, color), 0)[1], 0)
        if turn + 1 < HALVES:
            send_z(turn + 1, color)

    def sum_up(pair):
        mask = parity_mask(radial)
        even = jnp.zeros((8, radial), jnp.float32)
        odd = jnp.zeros((8, radial), jnp.float32)
        for row in range(0, depth, 8):
            red = field[0, pair, pl.ds(row + PAD, 8), :]
            black = field[1, pair, pl.ds(row + PAD, 8), :]
            even += jnp.where(mask, red, black)
            odd += jnp.where(mask, black, red)
        total[pair, pl.ds(0, 1), :] = jnp.sum(even, axis=0, keepdims=True)
        total[pair, pl.ds(1, 1), :] = jnp.sum(odd, axis=0, keepdims=True)

    lax.fori_loop(1, pairs + 1, lambda a, _: (sum_up(a), 0)[1], 0)
    for side in range(2):
        take_j(HALVES, 1, side)
    sum_up(0)
    sum_up(pairs + 1)

    def tcopy(step):
        return pltpu.make_async_remote_copy(
            src_ref=total,
            dst_ref=total_recv.at[step - 1],
            send_sem=tsend_sem.at[step - 1],
            recv_sem=trecv_sem.at[step - 1],
            device_id={"gz": lax.rem(slab + step, slabs)},
            device_id_type=MESH,
        )

    for step in range(1, slabs):
        tcopy(step).start()
    beyond = jnp.zeros(carry.shape, jnp.float32)
    for step in range(1, slabs):
        tcopy(step).wait_recv()
        beyond = beyond + jnp.where(step > slab, total_recv[step - 1], 0.0)
    carry[...] = beyond

    for step in range(1, slabs):
        tcopy(step).wait_send()
    for turn in range(HALVES + 1):
        for side in range(2):
            jcopy(turn, side).wait_send()
    for turn in range(HALVES):
        @pl.when(has_next)
        def _():
            zcopy(turn, 0).wait_send()

        @pl.when(has_prev)
        def _():
            zcopy(turn, 1).wait_send()


def drift_kernel(coef, field, carry, potential, shift_r, shift_phi, sums):
    step = pl.program_id(0)
    depth, radial = potential.shape[1], potential.shape[2]
    mask = parity_mask(radial)
    row = lax.broadcasted_iota(jnp.int32, (8, radial), 0)
    slot = lax.rem(step, 3)
    for side in range(2):
        run = jnp.broadcast_to(carry[0, pl.ds(side, 1), :], (8, radial))
        for at in range(depth - 8, -8, -8):
            red = field[0, 0, pl.ds(at + PAD, 8), :]
            black = field[1, 0, pl.ds(at + PAD, 8), :]
            part = jnp.where(mask, red, black) if side == 0 else jnp.where(mask, black, red)
            for hop in (1, 2, 4):
                part = part + jnp.where(row < 8 - hop, pltpu.roll(part, 8 - hop, axis=0), 0.0)
            part = part + run
            sums[slot, side, pl.ds(at, 8), :] = part
            run = jnp.broadcast_to(part[0:1, :], (8, radial))

    @pl.when(step >= 2)
    def _():
        mid, low = lax.rem(step + 2, 3), lax.rem(step + 1, 3)
        out_c, in_c, phi_c = coef[4], coef[5], coef[6]
        for at in range(0, depth, 8):
            rows = pl.ds(at, 8)
            planes = (sums[low, 1, rows, :], sums[mid, 0, rows, :], sums[mid, 1, rows, :], sums[slot, 0, rows, :])
            for side in range(2):
                here = planes[side + 1]
                along_r = out_c * pltpu.roll(here, radial - 1, axis=1) + in_c * pltpu.roll(here, 1, axis=1)
                along_phi = phi_c * (planes[side + 2] - planes[side])
                shift_r[side, rows, :] = along_r + 0.3 * along_phi
                shift_phi[side, rows, :] = along_phi - 0.3 * along_r


def coefficients(radial, sectors):
    radius = radial * 0.5 + np.arange(radial, dtype=np.float64) + 0.5
    step_phi = 2.0 * math.pi / sectors
    around = 1.0 / (radius * step_phi) ** 2
    diag = 4.0 + 2.0 * around
    has_next = np.arange(radial) < radial - 1
    has_prev = np.arange(radial) > 0
    drift = 1.0 / (1.09 * 32.0)
    rows = [
        RELAX * (1.0 + 0.5 / radius) / diag * has_next,
        RELAX * (1.0 - 0.5 / radius) / diag * has_prev,
        RELAX * around / diag,
        RELAX / diag,
        -0.5 * drift * has_next,
        0.5 * drift * has_prev,
        -0.5 * drift / (radius * step_phi),
        np.zeros(radial),
    ]
    stacked = np.stack(rows).astype(np.float32)
    return jnp.asarray(np.ascontiguousarray(np.broadcast_to(stacked[:, None, :], (8, 8, radial))))


def local(slabs, rings, potential_in, charge, cell_kind):
    sectors, depth, radial = potential_in.shape
    pairs = sectors // 2
    tall = depth + 2 * PAD
    coef = coefficients(radial, sectors * rings)
    any_spec = pl.BlockSpec(memory_space=pl.ANY)
    vmem_spec = pl.BlockSpec(memory_space=pltpu.VMEM)
    chunks = 2 + -(-(pairs - 2) // LOAD_PAIRS)
    f32 = jnp.float32
    field, carry = pl.pallas_call(
        functools.partial(relax_kernel, slabs, rings),
        out_shape=(
            jax.ShapeDtypeStruct((2, pairs + 2, tall, radial), f32),
            jax.ShapeDtypeStruct((pairs + 2, 2, radial), f32),
        ),
        in_specs=[any_spec, any_spec, any_spec, vmem_spec],
        out_specs=(vmem_spec, vmem_spec),
        scratch_shapes=[
            pltpu.VMEM((sectors, depth, radial), f32),
            pltpu.VMEM((sectors, depth, radial), f32),
            pltpu.VMEM((sectors, depth, radial), jnp.int32),
            pltpu.VMEM((2, pairs, depth, radial), f32),
            pltpu.VMEM((HALVES + 1, 2, depth // 2, radial), f32),
            pltpu.VMEM((HALVES + 1, 2, depth // 2, radial), f32),
            pltpu.VMEM((HALVES, 2, pairs, 1, radial), f32),
            pltpu.VMEM((HALVES, 2, pairs, 1, radial), f32),
            pltpu.VMEM((pairs + 2, 2, radial), f32),
            pltpu.VMEM((slabs - 1, pairs + 2, 2, radial), f32),
            pltpu.SemaphoreType.DMA((chunks, 3)),
            pltpu.SemaphoreType.DMA((HALVES + 1, 2)),
            pltpu.SemaphoreType.DMA((HALVES + 1, 2)),
            pltpu.SemaphoreType.DMA((HALVES, 2)),
            pltpu.SemaphoreType.DMA((HALVES, 2)),
            pltpu.SemaphoreType.DMA((slabs - 1,)),
            pltpu.SemaphoreType.DMA((slabs - 1,)),
        ],
        compiler_params=pltpu.CompilerParams(collective_id=0, has_side_effects=True),
    )(potential_in, charge, cell_kind, coef)

    block = jax.ShapeDtypeStruct((sectors, depth, radial), f32)

    def out_map(g):
        return (jnp.maximum(g - 2, 0), 0, 0)

    return pl.pallas_call(
        drift_body,
        out_shape=(block, block, block),
        grid=(pairs + 2,),
        in_specs=[
            pl.BlockSpec((8, 8, radial), lambda g: (0, 0, 0)),
            pl.BlockSpec((2, 1, tall, radial), lambda g: (0, g, 0, 0)),
            pl.BlockSpec((1, 2, radial), lambda g: (g, 0, 0)),
        ],
        out_specs=(pl.BlockSpec((2, depth, radial), lambda g: (jnp.clip(g - 1, 0, pairs - 1), 0, 0)),)
        + (pl.BlockSpec((2, depth, radial), out_map),) * 2,
        scratch_shapes=[pltpu.VMEM((3, 2, depth, radial), f32)],
    )(coef, field, carry)


def drift_body(coef, field, carry, potential, shift_r, shift_phi, sums):
    step = pl.program_id(0)
    depth, radial = potential.shape[1], potential.shape[2]

    @pl.when(jnp.logical_and(step >= 1, step < pl.num_programs(0) - 1))
    def _():
        mask = parity_mask(radial)
        for at in range(0, depth, 8):
            red = field[0, 0, pl.ds(at + PAD, 8), :]
            black = field[1, 0, pl.ds(at + PAD, 8), :]
            potential[0, pl.ds(at, 8), :] = jnp.where(mask, red, black)
            potential[1, pl.ds(at, 8), :] = jnp.where(mask, black, red)

    drift_kernel(coef, field, carry, potential, shift_r, shift_phi, sums)


def solution(mesh):
    spec = P("phi", "gz", None)
    body = functools.partial(local, mesh.shape["gz"], mesh.shape["phi"])
    return jax.shard_map(body, mesh=mesh, in_specs=(spec,) * 3, out_specs=(spec,) * 3, check_vma=False)
```

profile of v0, /device:TPU:0, one launch (start us, length us, event | category | flops | bytes accessed | tf_op | source)
XLA Modules:
  0.0 71.1 jit_solution(6975077860615281359)
XLA Ops:
  0.6 55.3 %shard_map.67 = (f32[2,18,144,256]{3,2,1,0:T(8,128)}, f32[18,2,256]{2,1,0:T(2,128)}) custom-call(f32[32,128,256]{2,1,0:T(8,128)} %pot.1, f32[32,128,256]{2,1,0:T(8,128)} %chg.1, s32[32,128,256]{2,1,0:T(8,128)} %kind.1, f32[8,8,256]{2,1,0:T(8,128)} %constant.2.clone.coef), custom_call_target="tpu_custom_call" | custom-call | tf_op jit(solution)/shard_map/pallas_call | solution.py:323
  55.9 15.2 %shard_map.68 = (f32[32,128,256]{2,1,0:T(8,128)}, f32[32,128,256]{2,1,0:T(8,128)}, f32[32,128,256]{2,1,0:T(8,128)}) custom-call(f32[8,8,256]{2,1,0:T(8,128)} %constant.2.clone.coef, f32[2,18,144,256]{3,2,1,0:T(8,128)} %get-tuple-element.5.field, f32[18,2,256]{2,1,0:T(2,128)} %get-tuple-element.6.carry), custom_call_target="tpu_custom_call" | custom-call | tf_op jit(solution)/shard_map/pallas_call | solution.py:358
where the time goes:
time: 71.6 us; the launch traced here: 71.1 us
  Pallas kernels  70.5 us (98%)
    pallas_call x1, Pallas kernels, local(): pl.pallas_call(functools.partial(relax_kernel, slabs, rings), out_shape=(...  55.3 us
    pallas_call x1, Pallas kernels, local(): pl.pallas_call(drift_body, out_shape=(block, block, block), grid=(pairs +...  15.2 us

commit v1 on v0

--- a/solution.py
+++ b/solution.py
@@ -148,12 +148,12 @@
             for pair in range(pairs):
                 field[color, pair + 1, pl.ds(PAD + depth, 1), :] = zrecv[turn, 1, pair]
 
-    def update(pair, color):
+    def update(pair, color, blocks):
         other = 1 - color
         mask = parity_mask(radial)
         out_c, in_c, around_c, z_c = coef[0], coef[1], coef[2], coef[3]
         before, after = (pair - 1, pair + 1) if color == 0 else (pair + 1, pair - 1)
-        for row in range(0, depth, 8):
+        for row in blocks:
             rows = pl.ds(row + PAD, 8)
             own = field[color, pair, rows, :]
             near = field[other, pair, rows, :]
@@ -193,17 +193,20 @@
         lax.fori_loop(first, first + count, lambda a, _: (prepare(a), 0)[1], 0)
     send_z(0, 1)
 
+    whole, ends, inner = range(0, depth, 8), (0, depth - 8), range(8, depth - 8, 8)
     for turn in range(HALVES):
         color = turn % 2
         take_z(turn, 1 - color)
         for side in range(2):
             take_j(turn, 1 - color, side)
-        for side in range(2):
-            update((pairs, 1)[side], color)
-            send_j(turn + 1, color, side)
-        lax.fori_loop(2, pairs, lambda a, _: (update(a, color), 0)[1], 0)
+            update((1, pairs)[side], color, whole)
+            send_j(turn + 1, color, 1 - side)
         if turn + 1 < HALVES:
+            lax.fori_loop(2, pairs, lambda a, _: (update(a, color, ends), 0)[1], 0)
             send_z(turn + 1, color)
+            lax.fori_loop(2, pairs, lambda a, _: (update(a, color, inner), 0)[1], 0)
+        else:
+            lax.fori_loop(2, pairs, lambda a, _: (update(a, color, whole), 0)[1], 0)
 
     def sum_up(pair):
         mask = parity_mask(radial)
@@ -262,17 +265,16 @@
     mask = parity_mask(radial)
     row = lax.broadcasted_iota(jnp.int32, (8, radial), 0)
     slot = lax.rem(step, 3)
-    for side in range(2):
-        run = jnp.broadcast_to(carry[0, pl.ds(side, 1), :], (8, radial))
-        for at in range(depth - 8, -8, -8):
-            red = field[0, 0, pl.ds(at + PAD, 8), :]
-            black = field[1, 0, pl.ds(at + PAD, 8), :]
+    runs = [jnp.broadcast_to(carry[0, pl.ds(side, 1), :], (8, radial)) for side in range(2)]
+    for at in range(depth - 8, -8, -8):
+        red = field[0, 0, pl.ds(at + PAD, 8), :]
+        black = field[1, 0, pl.ds(at + PAD, 8), :]
+        for side in range(2):
             part = jnp.where(mask, red, black) if side == 0 else jnp.where(mask, black, red)
             for hop in (1, 2, 4):
                 part = part + jnp.where(row < 8 - hop, pltpu.roll(part, 8 - hop, axis=0), 0.0)
-            part = part + run
-            sums[slot, side, pl.ds(at, 8), :] = part
-            run = jnp.broadcast_to(part[0:1, :], (8, radial))
+            sums[slot, side, pl.ds(at, 8), :] = part + runs[side]
+            runs[side] = runs[side] + jnp.broadcast_to(part[0:1, :], (8, radial))
 
     @pl.when(step >= 2)
     def _():

time: 71.6 us -> 62.3 us (0.87)
  Pallas kernels: 70.5 us -> 61.1 us
    pallas_call x1, Pallas kernels: 55.3 us -> 45.9 us  [local(): pl.pallas_call(functools.partial(relax_kernel, slabs, rings), out_shape=(...]
where the time goes in v1:
time: 62.3 us; the launch traced here: 61.8 us
  Pallas kernels  61.1 us (98%)
  between operations  0.64 us (1%)
    pallas_call x1, Pallas kernels, local(): pl.pallas_call(functools.partial(relax_kernel, slabs, rings), out_shape=(...  45.9 us
    pallas_call x1, Pallas kernels, local(): pl.pallas_call(drift_body, out_shape=(block, block, block), grid=(pairs +...  15.2 us

profile of v1, /device:TPU:0, one launch (start us, length us, event | category | flops | bytes accessed | tf_op | source)
XLA Modules:
  0.0 61.8 jit_solution(13456183018384340223)
XLA Ops:
  0.6 45.9 %shard_map.67 = (f32[2,18,144,256]{3,2,1,0:T(8,128)}, f32[18,2,256]{2,1,0:T(2,128)}) custom-call(f32[32,128,256]{2,1,0:T(8,128)} %pot.1, f32[32,128,256]{2,1,0:T(8,128)} %chg.1, s32[32,128,256]{2,1,0:T(8,128)} %kind.1, f32[8,8,256]{2,1,0:T(8,128)} %constant.2.clone.coef), custom_call_target="tpu_custom_call" | custom-call | tf_op jit(solution)/shard_map/pallas_call | solution.py:325
  46.5 15.2 %shard_map.68 = (f32[32,128,256]{2,1,0:T(8,128)}, f32[32,128,256]{2,1,0:T(8,128)}, f32[32,128,256]{2,1,0:T(8,128)}) custom-call(f32[8,8,256]{2,1,0:T(8,128)} %constant.2.clone.coef, f32[2,18,144,256]{3,2,1,0:T(8,128)} %get-tuple-element.5.field, f32[18,2,256]{2,1,0:T(2,128)} %get-tuple-element.6.carry), custom_call_target="tpu_custom_call" | custom-call | tf_op jit(solution)/shard_map/pallas_call | solution.py:360
